TPU v7x, 32 devices: a whole 2x2x4 slice. The times are simulated.
32 devices in a mesh: grp: 4 (over y, core), seq: 8 (over z, x).
Axes of the slice: x: 2, y: 2, z: 4, core: 2. Of those that a mesh axis runs over, the one named last changes fastest.
Arguments:
- tokens: bfloat16 [4, 2048, 2048], P('grp', 'seq'), may hold values from -6 to 6
- cotangent: bfloat16 [4, 2048, 2048], P('grp', 'seq'), may hold values from -6 to 6
- route_ids: int32 [4, 2048, 8], P('grp', 'seq'), may hold values from 0 to 15, all different within a row; in each aligned block of 256 rows (0 to 255, 256 to 511, ..., all dimensions but the last counted through in order) at most 144 rows name the same one
- gain_attn: bfloat16 [2048], P(('grp', 'seq')), may hold values from 0.099609375 to 1.8984375
- w_query: bfloat16 [2048, 2048], P(('grp', 'seq')), may hold values from -0.125 to 0.125
- w_key: bfloat16 [2048, 2048], P(('grp', 'seq')), may hold values from -0.125 to 0.125
- w_value: bfloat16 [2048, 2048], P(('grp', 'seq')), may hold values from -0.125 to 0.125
- w_out: bfloat16 [2048, 2048], P(('grp', 'seq')), may hold values from -1.5 to 1.5
- gain_query: bfloat16 [2048], P(('grp', 'seq')), may hold values from 0.099609375 to 1.8984375
- gain_key: bfloat16 [2048], P(('grp', 'seq')), may hold values from 0.099609375 to 1.8984375
- gain_ffn: bfloat16 [2048], P(('grp', 'seq')), may hold values from 0.099609375 to 1.8984375
- router: bfloat16 [2048, 16], P(('grp', 'seq')), may hold values from -0.125 to 0.125
- expert_gate: bfloat16 [16, 2048, 1024], P('seq', 'grp'), may hold values from -0.125 to 0.125
- expert_up: bfloat16 [16, 2048, 1024], P('seq', 'grp'), may hold values from -0.125 to 0.125
- expert_down: bfloat16 [16, 1024, 2048], P('seq', 'grp'), may hold values from -1.5 to 1.5
- clip_flags: int32 [16], replicated, may hold values from 0 to 1
- clip_factors: float32 [16], replicated, may hold values from 0.25 to 1
Outputs:
- block_out: bfloat16 [4, 2048, 2048], P('grp', 'seq')
- tokens_grad: float32 [4, 2048, 2048], P('grp', 'seq')
- gain_attn_grad: float32 [2048], P(('grp', 'seq'))
- w_query_grad: float32 [2048, 2048], P(('grp', 'seq'))
- w_key_grad: float32 [2048, 2048], P(('grp', 'seq'))
- w_value_grad: float32 [2048, 2048], P(('grp', 'seq'))
- w_out_grad: float32 [2048, 2048], P(('grp', 'seq'))
- gain_query_grad: float32 [2048], P(('grp', 'seq'))
- gain_key_grad: float32 [2048], P(('grp', 'seq'))
- gain_ffn_grad: float32 [2048], P(('grp', 'seq'))
- router_grad: float32 [2048, 16], P(('grp', 'seq'))
- expert_gate_grad: float32 [16, 2048, 1024], P('seq', 'grp')
- expert_up_grad: float32 [16, 2048, 1024], P('seq', 'grp')
- expert_down_grad: float32 [16, 1024, 2048], P('seq', 'grp')
- max_logit: float32 [16], replicated
- clipped_query: bfloat16 [2048, 2048], P(('grp', 'seq'))
- clipped_key: bfloat16 [2048, 2048], P(('grp', 'seq'))
Inputs may be any that keep to these rules, and one draw needn't show every extreme that they name: `route_ids`: each row names 8 different experts. In every aligned block of 256 rows of one group (the rows of one group on one index of seq) no expert is named by more than 144 rows, and in some blocks one expert is named by exactly 144 rows.
All inputs are finite; a program needn't handle non-finite values.
Results may differ from a plain program's by a relative error of at most 0.023.
Values may be sent and summed in bfloat16 or wider, within the bound.
A program may use at most 384 MiB of HBM per device.

v0:
```python
import jax
import jax.numpy as jnp
from jax import lax
from jax.sharding import PartitionSpec as P

D = 2048
H = 16
HD = 128
TOP = 8
E = 16
PROMPT = 1024
CONT_LEN = 128
GROUP_TOK = 2048


EPSILON = 1e-05
PRECISE = lax.Precision.HIGHEST


def normalize(values):
    factor = lax.rsqrt(jnp.mean(values * values, axis=-1, keepdims=True) + EPSILON)
    return (values * factor, factor)


def norm_back(grad_normed, normed, factor):
    return factor * (grad_normed - normed * jnp.mean(grad_normed * normed, axis=-1, keepdims=True))


def rotary_tables(position):
    inverse_freq = 10000.0 ** (-(jnp.arange(HD // 2, dtype=jnp.float32) * 2.0) / HD)
    phase_angle = position.astype(jnp.float32)[:, None] * inverse_freq[None, :]
    cosine_table = jnp.concatenate([jnp.cos(phase_angle), jnp.cos(phase_angle)], axis=-1)[
        :, None, :
    ]
    sine_table = jnp.concatenate([jnp.sin(phase_angle), jnp.sin(phase_angle)], axis=-1)[:, None, :]
    return (cosine_table, sine_table)


def rotate(values, cosine_table, sine_table, direction):
    front_half = values[..., : HD // 2]
    back_half = values[..., HD // 2 :]
    if direction > 0:
        turned = jnp.concatenate([-back_half, front_half], axis=-1)
    else:
        turned = jnp.concatenate([back_half, -front_half], axis=-1)
    return values * cosine_table + turned * sine_table


def per_device(
    tokens,
    cotangent,
    route_ids,
    gain_attn,
    w_query,
    w_key,
    w_value,
    w_out,
    gain_query,
    gain_key,
    gain_ffn,
    router,
    expert_gate,
    expert_up,
    expert_down,
    clip_flags,
    clip_factors,
):
    groups = tokens.shape[0]
    row_count = tokens.shape[1]
    capacity = 9 * row_count * TOP // (8 * E)
    shape4 = (groups, row_count, H, HD)
    score_scale = HD ** (-0.5)
    head_scale = jnp.where(clip_flags == 1, jnp.sqrt(clip_factors), jnp.ones_like(clip_factors))
    column_scale = jnp.broadcast_to(head_scale[:, None], (H, HD)).reshape(D)
    clipped_query = (w_query.astype(jnp.float32) * column_scale[None, :]).astype(jnp.bfloat16)
    clipped_key = (w_key.astype(jnp.float32) * column_scale[None, :]).astype(jnp.bfloat16)

    def fetch_attention():
        return (
            lax.all_gather(clipped_query, ("grp", "seq"), axis=0, tiled=True),
            lax.all_gather(clipped_key, ("grp", "seq"), axis=0, tiled=True),
            lax.all_gather(w_value, ("grp", "seq"), axis=0, tiled=True),
            lax.all_gather(w_out, ("grp", "seq"), axis=0, tiled=True),
            lax.all_gather(router, ("grp", "seq"), axis=0, tiled=True),
            lax.all_gather(gain_attn, ("grp", "seq"), axis=0, tiled=True),
            lax.all_gather(gain_query, ("grp", "seq"), axis=0, tiled=True),
            lax.all_gather(gain_key, ("grp", "seq"), axis=0, tiled=True),
            lax.all_gather(gain_ffn, ("grp", "seq"), axis=0, tiled=True),
        )

    def fetch_experts():
        return (
            lax.all_gather(expert_gate, "grp", axis=1, tiled=True),
            lax.all_gather(expert_up, "grp", axis=1, tiled=True),
            lax.all_gather(expert_down, "grp", axis=1, tiled=True),
        )

    global_rows = lax.axis_index("seq") * row_count + jnp.arange(row_count, dtype=jnp.int32)
    position = jnp.where(
        global_rows < PROMPT, global_rows, PROMPT + (global_rows - PROMPT) % CONT_LEN
    )
    cosine_table, sine_table = rotary_tables(position)
    prompt_rows = jnp.arange(PROMPT, dtype=jnp.int32)
    see_prompt = prompt_rows[None, :] <= global_rows[:, None]
    same_cont = (global_rows[None, :] - PROMPT) // CONT_LEN == (
        global_rows[:, None] - PROMPT
    ) // CONT_LEN
    see_local = (
        (global_rows[:, None] >= PROMPT)
        & same_cont
        & (global_rows[None, :] <= global_rows[:, None])
    )
    visible = jnp.concatenate([see_prompt, see_local], axis=1)
    fetched = fetch_attention()
    query_all, key_all, value_all, out_all, router_all = (
        fetched[0],
        fetched[1],
        fetched[2],
        fetched[3],
        fetched[4],
    )
    attn_gain = fetched[5].astype(jnp.float32)
    query_gain = fetched[6].astype(jnp.float32)
    key_gain = fetched[7].astype(jnp.float32)
    ffn_gain = fetched[8].astype(jnp.float32)
    inputs = tokens.astype(jnp.float32)
    normed_in, factor_in = normalize(inputs)
    hidden_in = (normed_in * attn_gain).astype(jnp.bfloat16)
    query_raw = jnp.einsum("grd,de->gre", hidden_in, query_all, preferred_element_type=jnp.float32)
    key_raw = jnp.einsum("grd,de->gre", hidden_in, key_all, preferred_element_type=jnp.float32)
    value_raw = jnp.einsum("grd,de->gre", hidden_in, value_all, preferred_element_type=jnp.float32)
    query_normed, query_factor = normalize(query_raw)
    key_normed, key_factor = normalize(key_raw)
    query_rot = rotate(
        (query_normed * query_gain).reshape(shape4), cosine_table, sine_table, 1
    ).astype(jnp.bfloat16)
    key_rot = rotate((key_normed * key_gain).reshape(shape4), cosine_table, sine_table, 1).astype(
        jnp.bfloat16
    )
    value_rows = value_raw.astype(jnp.bfloat16).reshape(shape4)

    def fetch_keys():
        whole_keys, whole_values = (
            lax.all_gather(key_rot, "seq", axis=1, tiled=True),
            lax.all_gather(value_rows, "seq", axis=1, tiled=True),
        )
        keys_cat = jnp.concatenate([whole_keys[:, :PROMPT], key_rot], axis=1)
        values_cat = jnp.concatenate([whole_values[:, :PROMPT], value_rows], axis=1)
        return (keys_cat, values_cat)

    def scores_of(keys_cat):
        raw_scores = (
            jnp.einsum("grhe,gkhe->ghrk", query_rot, keys_cat, preferred_element_type=jnp.float32)
            * score_scale
        )
        return jnp.where(visible[None, None], raw_scores, -1e30)

    keys_cat, values_cat = fetch_keys()
    masked = scores_of(keys_cat)
    row_peak = jnp.max(masked, axis=-1)
    row_total = jnp.sum(jnp.exp(masked - row_peak[..., None]), axis=-1)
    log_total = row_peak + jnp.log(row_total)
    probs_att = jnp.exp(masked - log_total[..., None])
    max_logit = lax.pmax(jnp.max(row_peak, axis=(0, 2)), ("grp", "seq"))
    attended = jnp.einsum(
        "ghrk,gkhe->grhe",
        probs_att.astype(jnp.bfloat16),
        values_cat,
        preferred_element_type=jnp.float32,
    )
    attended = attended.reshape(groups, row_count, D).astype(jnp.bfloat16)
    residual_mid = inputs + jnp.einsum(
        "grd,de->gre", attended, out_all, preferred_element_type=jnp.float32
    )
    normed_mid, factor_mid = normalize(residual_mid)
    hidden_mid = (normed_mid * ffn_gain).astype(jnp.bfloat16)
    logits = jnp.einsum("grd,de->gre", hidden_mid, router_all, preferred_element_type=jnp.float32)
    gate_prob = jax.nn.softmax(logits, axis=-1)
    expert_ids = jnp.arange(E, dtype=jnp.int32)
    onehot = (route_ids[..., None] == expert_ids).astype(jnp.int32)
    flat_hot = onehot.reshape(groups, row_count * TOP, E)
    before = jnp.cumsum(flat_hot, axis=1, dtype=jnp.int32) - flat_hot
    slot_place = jnp.sum(before * flat_hot, axis=2, dtype=jnp.int32)
    group_ids = jnp.arange(groups, dtype=jnp.int32)[:, None]
    slot_index = (
        (route_ids.reshape(groups, row_count * TOP) * groups + group_ids) * capacity + slot_place
    ).reshape(-1)
    route_index = jnp.arange(groups * row_count * TOP, dtype=jnp.int32)
    slot_table = jnp.zeros((E * groups * capacity,), jnp.int32).at[slot_index].set(route_index + 1)
    filled = slot_table > 0
    route_of_slot = jnp.where(filled, slot_table - 1, 0)
    token_of_slot = route_of_slot // TOP
    onehot_float = onehot.astype(jnp.float32)
    route_weight = jnp.sum(onehot_float * gate_prob[:, :, None, :], axis=-1)
    hidden_flat = hidden_mid.reshape(groups * row_count, D)
    send_rows = jnp.where(
        filled[:, None], hidden_flat[token_of_slot], jnp.zeros((), jnp.bfloat16)
    ).reshape(E, groups * capacity, D)
    received = lax.all_to_all(send_rows, "seq", split_axis=0, concat_axis=1, tiled=True)
    gate_w, up_w, down_w = fetch_experts()
    gate_val = jnp.einsum("emd,edf->emf", received, gate_w, preferred_element_type=jnp.float32)
    up_val = jnp.einsum("emd,edf->emf", received, up_w, preferred_element_type=jnp.float32)
    sigmoid_gate = jax.nn.sigmoid(gate_val)
    silu_gate = gate_val * sigmoid_gate
    hidden = (silu_gate * up_val).astype(jnp.bfloat16)
    expert_out = jnp.einsum(
        "emf,efd->emd", hidden, down_w, preferred_element_type=jnp.float32
    ).astype(jnp.bfloat16)
    returned = lax.all_to_all(expert_out, "seq", split_axis=1, concat_axis=0, tiled=True).reshape(
        E * groups * capacity, D
    )
    route_out = returned[slot_index].reshape(groups, row_count, TOP, D)
    ffn_out = jnp.sum(route_weight[..., None] * route_out.astype(jnp.float32), axis=2)
    block_out = (residual_mid + ffn_out).astype(jnp.bfloat16)
    fetched = fetch_attention()
    query_all, key_all, value_all, out_all, router_all = (
        fetched[0],
        fetched[1],
        fetched[2],
        fetched[3],
        fetched[4],
    )
    gate_w, up_w, down_w = fetch_experts()
    grad_out = cotangent.astype(jnp.float32)
    grad_weight = jnp.sum(grad_out[:, :, None, :] * route_out.astype(jnp.float32), axis=-1)
    grad_flat = grad_out.reshape(groups * row_count, D)
    weight_flat = route_weight.reshape(-1)
    send_grads = jnp.where(
        filled[:, None], weight_flat[route_of_slot][:, None] * grad_flat[token_of_slot], 0.0
    )
    send_grads = send_grads.astype(jnp.bfloat16).reshape(E, groups * capacity, D)
    grad_received = lax.all_to_all(send_grads, "seq", split_axis=0, concat_axis=1, tiled=True)
    grad_hidden = jnp.einsum(
        "emd,efd->emf", grad_received, down_w, preferred_element_type=jnp.float32
    )
    grad_gate = (
        grad_hidden * up_val * sigmoid_gate * (1.0 + gate_val * (1.0 - sigmoid_gate))
    ).astype(jnp.bfloat16)
    grad_up = (grad_hidden * silu_gate).astype(jnp.bfloat16)
    grad_down_w = jnp.einsum(
        "emf,emd->efd", hidden, grad_received, preferred_element_type=jnp.float32
    )
    grad_gate_w = jnp.einsum(
        "emd,emf->edf", received, grad_gate, preferred_element_type=jnp.float32
    )
    grad_up_w = jnp.einsum("emd,emf->edf", received, grad_up, preferred_element_type=jnp.float32)
    grad_rows = jnp.einsum("emf,edf->emd", grad_gate, gate_w, preferred_element_type=jnp.float32)
    grad_rows = (
        grad_rows + jnp.einsum("emf,edf->emd", grad_up, up_w, preferred_element_type=jnp.float32)
    ).astype(jnp.bfloat16)
    back_rows = lax.all_to_all(grad_rows, "seq", split_axis=1, concat_axis=0, tiled=True).reshape(
        E * groups * capacity, D
    )
    expert_shares = (
        lax.psum_scatter(
            grad_gate_w.astype(jnp.bfloat16), "grp", scatter_dimension=1, tiled=True
        ).astype(jnp.float32),
        lax.psum_scatter(
            grad_up_w.astype(jnp.bfloat16), "grp", scatter_dimension=1, tiled=True
        ).astype(jnp.float32),
        lax.psum_scatter(
            grad_down_w.astype(jnp.bfloat16), "grp", scatter_dimension=1, tiled=True
        ).astype(jnp.float32),
    )
    grad_hidden_mid = jnp.sum(
        back_rows[slot_index].reshape(groups, row_count, TOP, D).astype(jnp.float32), axis=2
    )
    grad_prob = jnp.sum(onehot_float * grad_weight[..., None], axis=2)
    grad_logits = gate_prob * (grad_prob - jnp.sum(gate_prob * grad_prob, axis=-1, keepdims=True))
    grad_router = jnp.einsum(
        "grd,gre->de", hidden_mid.astype(jnp.float32), grad_logits, precision=PRECISE
    )
    grad_hidden_mid = grad_hidden_mid + jnp.einsum(
        "gre,de->grd", grad_logits, router_all.astype(jnp.float32), precision=PRECISE
    )
    grad_ffn_gain = jnp.sum(grad_hidden_mid * normed_mid, axis=(0, 1))
    grad_mid = grad_out + norm_back(grad_hidden_mid * ffn_gain, normed_mid, factor_mid)
    grad_attn = grad_mid.astype(jnp.bfloat16)
    grad_out_w = jnp.einsum("grd,gre->de", attended, grad_attn, preferred_element_type=jnp.float32)
    grad_attended = (
        jnp.einsum("gre,de->grd", grad_attn, out_all, preferred_element_type=jnp.float32)
        .astype(jnp.bfloat16)
        .reshape(shape4)
    )
    keys_cat, values_cat = fetch_keys()
    masked = scores_of(keys_cat)
    probs_att = jnp.exp(masked - log_total[..., None])
    grad_probs = jnp.einsum(
        "grhe,gkhe->ghrk", grad_attended, values_cat, preferred_element_type=jnp.float32
    )
    delta = jnp.sum(probs_att * grad_probs, axis=-1, keepdims=True)
    grad_scores = (probs_att * (grad_probs - delta)).astype(jnp.bfloat16)
    grad_query = (
        jnp.einsum("ghrk,gkhe->grhe", grad_scores, keys_cat, preferred_element_type=jnp.float32)
        * score_scale
    )
    grad_keys = (
        jnp.einsum("ghrk,grhe->gkhe", grad_scores, query_rot, preferred_element_type=jnp.float32)
        * score_scale
    )
    grad_values = jnp.einsum(
        "ghrk,grhe->gkhe",
        probs_att.astype(jnp.bfloat16),
        grad_attended,
        preferred_element_type=jnp.float32,
    )
    zero_rows = jnp.zeros((groups, GROUP_TOK - PROMPT, H, HD), jnp.float32)
    summed_keys, summed_values = (
        lax.psum_scatter(
            jnp.concatenate([grad_keys[:, :PROMPT], zero_rows], axis=1).astype(jnp.bfloat16),
            "seq",
            scatter_dimension=1,
            tiled=True,
        ).astype(jnp.float32),
        lax.psum_scatter(
            jnp.concatenate([grad_values[:, :PROMPT], zero_rows], axis=1).astype(jnp.bfloat16),
            "seq",
            scatter_dimension=1,
            tiled=True,
        ).astype(jnp.float32),
    )
    grad_key = summed_keys + grad_keys[:, PROMPT:]
    grad_value = summed_values + grad_values[:, PROMPT:]
    grad_query_h = rotate(grad_query, cosine_table, sine_table, -1).reshape(groups, row_count, D)
    grad_key_h = rotate(grad_key, cosine_table, sine_table, -1).reshape(groups, row_count, D)
    grad_query_gain = jnp.sum(grad_query_h * query_normed, axis=(0, 1))
    grad_key_gain = jnp.sum(grad_key_h * key_normed, axis=(0, 1))
    grad_query_raw = norm_back(grad_query_h * query_gain, query_normed, query_factor).astype(
        jnp.bfloat16
    )
    grad_key_raw = norm_back(grad_key_h * key_gain, key_normed, key_factor).astype(jnp.bfloat16)
    grad_value_raw = grad_value.reshape(groups, row_count, D).astype(jnp.bfloat16)
    grad_query_w = (
        jnp.einsum("grd,gre->de", hidden_in, grad_query_raw, preferred_element_type=jnp.float32)
        * column_scale[None, :]
    )
    grad_key_w = (
        jnp.einsum("grd,gre->de", hidden_in, grad_key_raw, preferred_element_type=jnp.float32)
        * column_scale[None, :]
    )
    grad_value_w = jnp.einsum(
        "grd,gre->de", hidden_in, grad_value_raw, preferred_element_type=jnp.float32
    )
    grad_hidden_in = jnp.einsum(
        "gre,de->grd", grad_query_raw, query_all, preferred_element_type=jnp.float32
    )
    grad_hidden_in = grad_hidden_in + jnp.einsum(
        "gre,de->grd", grad_key_raw, key_all, preferred_element_type=jnp.float32
    )
    grad_hidden_in = grad_hidden_in + jnp.einsum(
        "gre,de->grd", grad_value_raw, value_all, preferred_element_type=jnp.float32
    )
    grad_attn_gain = jnp.sum(grad_hidden_in * normed_in, axis=(0, 1))
    tokens_grad = grad_mid + norm_back(grad_hidden_in * attn_gain, normed_in, factor_in)
    shares = (
        lax.psum_scatter(grad_query_w, ("grp", "seq"), scatter_dimension=0, tiled=True),
        lax.psum_scatter(grad_key_w, ("grp", "seq"), scatter_dimension=0, tiled=True),
        lax.psum_scatter(grad_value_w, ("grp", "seq"), scatter_dimension=0, tiled=True),
        lax.psum_scatter(grad_out_w, ("grp", "seq"), scatter_dimension=0, tiled=True),
        lax.psum_scatter(grad_router, ("grp", "seq"), scatter_dimension=0, tiled=True),
        lax.psum_scatter(grad_attn_gain, ("grp", "seq"), scatter_dimension=0, tiled=True),
        lax.psum_scatter(grad_query_gain, ("grp", "seq"), scatter_dimension=0, tiled=True),
        lax.psum_scatter(grad_key_gain, ("grp", "seq"), scatter_dimension=0, tiled=True),
        lax.psum_scatter(grad_ffn_gain, ("grp", "seq"), scatter_dimension=0, tiled=True),
    )
    return (
        block_out,
        tokens_grad,
        shares[5],
        shares[0],
        shares[1],
        shares[2],
        shares[3],
        shares[6],
        shares[7],
        shares[8],
        shares[4],
        expert_shares[0],
        expert_shares[1],
        expert_shares[2],
        max_logit,
        clipped_query,
        clipped_key,
    )


def solution(mesh):
    return jax.shard_map(
        per_device,
        mesh=mesh,
        in_specs=(
            P("grp", "seq", None),
            P("grp", "seq", None),
            P("grp", "seq", None),
            P(("grp", "seq")),
            P(("grp", "seq"), None),
            P(("grp", "seq"), None),
            P(("grp", "seq"), None),
            P(("grp", "seq"), None),
            P(("grp", "seq")),
            P(("grp", "seq")),
            P(("grp", "seq")),
            P(("grp", "seq"), None),
            P("seq", "grp", None),
            P("seq", "grp", None),
            P("seq", "grp", None),
            P(),
            P(),
        ),
        out_specs=(
            P("grp", "seq", None),
            P("grp", "seq", None),
            P(("grp", "seq")),
            P(("grp", "seq"), None),
            P(("grp", "seq"), None),
            P(("grp", "seq"), None),
            P(("grp", "seq"), None),
            P(("grp", "seq")),
            P(("grp", "seq")),
            P(("grp", "seq")),
            P(("grp", "seq"), None),
            P("seq", "grp", None),
            P("seq", "grp", None),
            P("seq", "grp", None),
            P(),
            P(("grp", "seq"), None),
            P(("grp", "seq"), None),
        ),
        check_vma=False,
    )
```

profile of v0, /device:TPU:0, one launch (start us, length us, event | category | flops | bytes accessed | tf_op | source)
XLA Modules:
  0.0 3930.2 jit_solution(7768437964539416284)
XLA Ops:
  15.5 42.6 %all-reduce.11 = (bf16[2048]{0:T(1024)(128)(2,1)S(1)}, bf16[2048]{0:T(1024)(128)(2,1)S(1)}, bf16[2048]{0:T(1024)(128)(2,1)S(1)}, bf16[2048]{0:T(1024)(128)(2,1)S(1)}) all-reduce(bf16[2048]{0:T(1024)(128)(2,1)S(1)} %dynamic-update-slice, bf16[2048]{0:T(1024)(128)(2,1)S(1)} %dynamic-update-slice.1, ...), channel_id=1, replica_groups=mesh['grp'=4,'seq'=8] {'grp','seq'}, use_global_device_ids=true, to_apply=%add.2 | all-reduce | flops 8192 | bytes 32768
  61.1 30.3 all-gather.17.cloned.1.call-done
  103.0 67.0 %all-gather.11.cloned.1.call-done = bf16[2048,2048]{1,0:T(8,128)(2,1)} async-done(((bf16[64,2048]{1,0:T(8,128)(2,1)}), bf16[2048,2048]{1,0:T(8,128)(2,1)}) %all-gather.11.cloned.1.call-update) | async-done | bytes 8388624 | tf_op jit(solution)/shard_map/all_gather | solution.py:82
  195.6 53.8 %all-gather.15.cloned.1.call-done = bf16[2048,2048]{1,0:T(8,128)(2,1)} async-done(((bf16[64,2048]{1,0:T(8,128)(2,1)}), bf16[2048,2048]{1,0:T(8,128)(2,1)}) %all-gather.15.cloned.1.call-update) | async-done | bytes 8388624 | tf_op jit(solution)/shard_map/all_gather | solution.py:80
  261.9 112.7 %all-gather.19.cloned.1.call-done = bf16[1,2048,16,128]{3,1,2,0:T(8,128)(2,1)} async-done(((bf16[1,256,16,128]{3,1,2,0:T(8,128)(2,1)}), bf16[1,2048,16,128]{3,1,2,0:T(8,128)(2,1)}) %all-gather.19.cloned.1.call-update) | async-done | bytes 8388624 | tf_op jit(solution)/shard_map/all_gather | solution.py:144
  398.9 100.7 %all-gather.13.cloned.1.call-done = bf16[1,2048,16,128]{1,3,2,0:T(8,128)(2,1)} async-done(((bf16[1,256,16,128]{1,3,2,0:T(8,128)(2,1)}), bf16[1,2048,16,128]{1,3,2,0:T(8,128)(2,1)}) %all-gather.13.cloned.1.call-update) | async-done | bytes 8388624 | tf_op jit(solution)/shard_map/all_gather | solution.py:145
  513.6 64.1 %all-gather.21.cloned.1.call-done = bf16[2048,2048]{1,0:T(8,128)(2,1)} async-done(((bf16[64,2048]{1,0:T(8,128)(2,1)}), bf16[2048,2048]{1,0:T(8,128)(2,1)}) %all-gather.21.cloned.1.call-update) | async-done | bytes 8388624 | tf_op jit(solution)/shard_map/all_gather | solution.py:83
  618.4 205.4 %all-to-all-done = bf16[16,144,2048]{2,1,0:T(8,128)(2,1)} async-done(((bf16[16,144,2048]{2,1,0:T(8,128)(2,1)}), bf16[16,144,2048]{2,1,0:T(8,128)(2,1)}, u32[]{:S(2)}, u32[]{:S(2)}) %all-to-all-start) | async-done | bytes 9437216 | tf_op jit(solution)/shard_map/all_to_all | solution.py:199
  850.1 19.8 multiply_convert_fusion.3
  884.1 28.3 copy.173
  917.7 261.1 %all-gather = bf16[32,64,16]{1,2,0:T(8,128)(2,1)S(1)} all-gather(bf16[1,64,16]{1,2,0:T(8,128)(2,1)S(1)} %bitcast.253), channel_id=1, replica_groups=mesh['grp'=4,'seq'=8] {'grp','seq'}, dimensions={0}, use_global_device_ids=true | all-gather | bytes 67584 | tf_op jit(solution)/shard_map/all_gather | solution.py:84
  1204.8 21.2 gather_fusion.1
  1251.3 206.9 %all_to_all.66 = bf16[16,144,2048]{2,1,0:T(8,128)(2,1)} all-to-all(bf16[16,144,2048]{2,1,0:T(8,128)(2,1)S(1)} %select_convert_fusion), channel_id=1, replica_groups=mesh['grp'=4,'seq'=8] {'seq'}, dimensions={0} | all-to-all | bytes 18874368 | tf_op jit(solution)/shard_map/all_to_all | solution.py:232
  1467.4 21.2 multiply_convert_fusion.1
  1505.9 18.7 add_convert_fusion
  1524.6 18.2 copy.177
  1560.9 191.0 %all-to-all-done.3 = bf16[2,1152,2048]{2,0,1:T(2,128)(2,1)} async-done(((bf16[2,1152,2048]{2,0,1:T(2,128)(2,1)}), bf16[2,1152,2048]{2,0,1:T(2,128)(2,1)}, u32[]{:S(2)}, u32[]{:S(2)}) %all-to-all-start.3) | async-done | bytes 9437216 | tf_op jit(solution)/shard_map/all_to_all | solution.py:251
  1763.8 21.2 gather_fusion.4
  1845.3 18.2 multiply_convert_fusion
  1887.1 18.0 convolution_convert_fusion.1
  1949.7 23.1 reduce-scatter.15.cloned.1.call-done
  1997.7 125.7 %reduce-scatter.13.cloned.1.call-done = bf16[1,256,16,128]{3,1,2,0:T(8,128)(2,1)} async-done(((bf16[1,2048,16,128]{3,1,2,0:T(8,128)(2,1)}), bf16[1,256,16,128]{3,1,2,0:T(8,128)(2,1)}) %reduce-scatter.13.cloned.1.call-update) | async-done | bytes 1048592 | tf_op jit(solution)/shard_map/reduce_scatter | solution.py:309
  2158.3 103.7 %reduce-scatter.31.cloned.1.call-done = f32[64,16]{1,0:T(8,128)} async-done(((f32[2048,16]{1,0:T(8,128)}), f32[64,16]{1,0:T(8,128)}) %reduce-scatter.31.cloned.1.call-update) | async-done | bytes 4112
  2263.4 37.4 pmax.7
  2300.8 32.3 reduce-scatter.29.cloned.1.call-done
  2337.2 69.7 %reduce-scatter.25.cloned.1.call-done = bf16[2,512,1024]{2,1,0:T(8,128)(2,1)} async-done(((bf16[2,2048,1024]{2,1,0:T(8,128)(2,1)}), bf16[2,512,1024]{2,1,0:T(8,128)(2,1)}) %reduce-scatter.25.cloned.1.call-update) | async-done | bytes 2097168 | tf_op jit(solution)/shard_map/reduce_scatter | solution.py:255
  2411.0 69.8 %reduce-scatter.27.cloned.1.call-done = bf16[2,512,1024]{2,1,0:T(8,128)(2,1)} async-done(((bf16[2,2048,1024]{2,1,0:T(8,128)(2,1)}), bf16[2,512,1024]{2,1,0:T(8,128)(2,1)}) %reduce-scatter.27.cloned.1.call-update) | async-done | bytes 2097168 | tf_op jit(solution)/shard_map/reduce_scatter | solution.py:258
  2500.7 50.5 %all-reduce.10 = (f32[2048]{0:T(1024)S(1)}, f32[2048]{0:T(1024)S(1)}, f32[2048]{0:T(1024)S(1)}, f32[2048]{0:T(1024)S(1)}) all-reduce(f32[2048]{0:T(1024)S(1)} %get-tuple-element.25, f32[2048]{0:T(1024)S(1)} %get-tuple-element.23, f32[2048]{0:T(1024)S(1)} %get-tuple-element.21, ...), channel_id=4, replica_groups=mesh['grp'=4,'seq'=8] {'grp','seq'}, use_global_device_ids=true, to_apply=%region_26.27.clone | all-reduce | flops 8192 | bytes 65536
  2557.1 286.0 %reduce-scatter.23.cloned.1.call-done = f32[64,2048]{1,0:T(8,128)} async-done(((f32[2048,2048]{1,0:T(8,128)}), f32[64,2048]{1,0:T(8,128)}) %reduce-scatter.23.cloned.1.call-update) | async-done | bytes 524304 | tf_op jit(solution)/shard_map/reduce_scatter | solution.py:359
  2843.1 360.1 %reduce-scatter.21.cloned.1.call-done = f32[64,2048]{1,0:T(8,128)} async-done(((f32[2048,2048]{1,0:T(8,128)}), f32[64,2048]{1,0:T(8,128)}) %reduce-scatter.21.cloned.1.call-update) | async-done | bytes 524304 | tf_op jit(solution)/shard_map/reduce_scatter | solution.py:358
  3203.2 360.1 %reduce-scatter.19.cloned.1.call-done = f32[64,2048]{1,0:T(8,128)} async-done(((f32[2048,2048]{1,0:T(8,128)}), f32[64,2048]{1,0:T(8,128)}) %reduce-scatter.19.cloned.1.call-update) | async-done | bytes 524304 | tf_op jit(solution)/shard_map/reduce_scatter | solution.py:357
  3563.3 360.3 %reduce-scatter.17.cloned.1.call-done = f32[64,2048]{1,0:T(8,128)} async-done(((f32[2048,2048]{1,0:T(8,128)}), f32[64,2048]{1,0:T(8,128)}) %reduce-scatter.17.cloned.1.call-update) | async-done | bytes 524304 | tf_op jit(solution)/shard_map/reduce_scatter | solution.py:356
  (364 shorter events, 515.5 us)
Async XLA Ops:
  7.2 84.2 %all-gather.17.cloned.1.call-start = ((), (), s32[]{:S(2)}) async-start(), calls=%async_computation.17 | async-start | bytes 8650752 | tf_op jit(solution)/shard_map/all_gather | solution.py:81
  10.5 159.5 %all-gather.11.cloned.1.call-start = ((), (), s32[]{:S(2)}) async-start(), calls=%async_computation.14 | async-start | bytes 8650752 | tf_op jit(solution)/shard_map/all_gather | solution.py:82
  11.3 238.1 %all-gather.15.cloned.1.call-start = ((), (), s32[]{:S(2)}) async-start(), calls=%async_computation.16 | async-start | bytes 8650752 | tf_op jit(solution)/shard_map/all_gather | solution.py:80
  12.0 362.5 %all-gather.19.cloned.1.call-start = ((), (), s32[]{:S(2)}) async-start(), calls=%async_computation.18 | async-start | bytes 9437184 | tf_op jit(solution)/shard_map/all_gather | solution.py:144
  58.1 191.3 %copy-start.42 = (f32[2048]{0:T(1024)}, f32[2048]{0:T(1024)S(1)}, u32[]{:S(2)}) copy-start(f32[2048]{0:T(1024)S(1)} %convert_element_type.249) | copy-start | bytes 24580
  59.5 119.8 %copy-start.31 = (f32[256,128]{1,0:T(8,128)}, f32[256,128]{1,0:T(8,128)S(1)}, u32[]{:S(2)}) copy-start(f32[256,128]{1,0:T(8,128)S(1)} %get-tuple-element.52) | copy-start | bytes 393220
  59.5 119.9 %copy-start.33 = (f32[256,128]{1,0:T(8,128)}, f32[256,128]{1,0:T(8,128)S(1)}, u32[]{:S(2)}) copy-start(f32[256,128]{1,0:T(8,128)S(1)} %get-tuple-element.78) | copy-start | bytes 393220
  61.1 188.3 %copy-start.58 = (f32[256]{0:T(256)}, f32[256]{0:T(256)S(1)}, u32[]{:S(2)}) copy-start(f32[256]{0:T(256)S(1)} %add_rsqrt_fusion.3) | copy-start | bytes 3076
  103.0 396.6 %all-gather.13.cloned.1.call-start = ((), (), s32[]{:S(2)}) async-start(), calls=%async_computation.15 | async-start | bytes 9437184 | tf_op jit(solution)/shard_map/all_gather | solution.py:145
  177.2 400.5 %all-gather.21.cloned.1.call-start = ((), (), s32[]{:S(2)}) async-start(), calls=%async_computation.19 | async-start | bytes 8650752 | tf_op jit(solution)/shard_map/all_gather | solution.py:83
  177.8 655.3 %all-gather.23.cloned.1.call-start = ((), (), s32[]{:S(2)}) async-start(), calls=%async_computation.20 | async-start | bytes 10485760 | tf_op jit(solution)/shard_map/all_gather | solution.py:93
  178.5 671.6 %all-gather.25.cloned.1.call-start = ((), (), s32[]{:S(2)}) async-start(), calls=%async_computation.21 | async-start | bytes 10485760 | tf_op jit(solution)/shard_map/all_gather | solution.py:94
  193.9 389.7 %copy-start.54 = (f32[2048]{0:T(1024)}, f32[2048]{0:T(1024)S(1)}, u32[]{:S(2)}) copy-start(f32[2048]{0:T(1024)S(1)} %convert_element_type.268) | copy-start | bytes 24580
  194.0 401.1 %copy-start.61 = (pred[16,144]{1,0:T(8,128)(4,1)}, pred[16,144]{1,0:T(8,128)(4,1)S(1)}, u32[]{:S(2)}) copy-start(pred[16,144]{1,0:T(8,128)(4,1)S(1)} %broadcast_in_dim.43) | copy-start | bytes 6916
  261.8 115.3 %copy-start.24 = (bf16[1,256,16,128]{3,1,2,0:T(8,128)(2,1)S(1)}, bf16[1,256,16,128]{3,1,2,0:T(8,128)(2,1)}, u32[]{:S(2)}) copy-start(bf16[1,256,16,128]{3,1,2,0:T(8,128)(2,1)} %fusion.28) | copy-start | bytes 3145732
  261.9 115.3 %copy-start.29 = (bf16[256,16,128]{0,2,1:T(8,128)(2,1)S(1)}, bf16[256,16,128]{0,2,1:T(8,128)(2,1)}, u32[]{:S(2)}) copy-start(bf16[256,16,128]{0,2,1:T(8,128)(2,1)} %fusion.26) | copy-start | bytes 3145732
  261.9 115.3 %copy-start.41 = (pred[256,1280]{1,0:T(8,128)(4,1)S(1)}, pred[256,1280]{1,0:T(8,128)(4,1)}, u32[]{:S(2)}) copy-start(pred[256,1280]{1,0:T(8,128)(4,1)} %pad_add_fusion) | copy-start | bytes 983044
  585.1 606.9 %copy-start = (bf16[256,2048]{1,0:T(8,128)(2,1)}, bf16[256,2048]{1,0:T(8,128)(2,1)S(1)}, u32[]{:S(2)}) copy-start(bf16[256,2048]{1,0:T(8,128)(2,1)S(1)} %fusion.38) | copy-start | bytes 3145732
  603.2 220.7 %all-to-all-start = ((bf16[16,144,2048]{2,1,0:T(8,128)(2,1)}), bf16[16,144,2048]{2,1,0:T(8,128)(2,1)}, u32[]{:S(2)}, u32[]{:S(2)}) async-start(bf16[16,144,2048]{2,1,0:T(8,128)(2,1)} %broadcast_select_fusion), calls=%async_computation | async-start | bytes 18874368 | tf_op jit(solution)/shard_map/all_to_all | solution.py:199
  617.7 252.2 %all-gather.27.cloned.1.call-start = ((), (), s32[]{:S(2)}) async-start(), calls=%async_computation.22 | async-start | bytes 10485760 | tf_op jit(solution)/shard_map/all_gather | solution.py:95
  912.4 280.6 %all-to-all-start.1 = ((bf16[2,1152,2048]{2,0,1:T(2,128)(2,1)}), bf16[2,1152,2048]{2,0,1:T(2,128)(2,1)}, u32[]{:S(2)}, u32[]{:S(2)}) async-start(bf16[2,1152,2048]{2,0,1:T(2,128)(2,1)} %copy.173), calls=%async_computation.1 | async-start | bytes 18874368 | tf_op jit(solution)/shard_map/all_to_all | solution.py:209
  1542.9 209.1 %all-to-all-start.3 = ((bf16[2,1152,2048]{2,0,1:T(2,128)(2,1)}), bf16[2,1152,2048]{2,0,1:T(2,128)(2,1)}, u32[]{:S(2)}, u32[]{:S(2)}) async-start(bf16[2,1152,2048]{2,0,1:T(2,128)(2,1)} %copy.177), calls=%async_computation.3 | async-start | bytes 18874368 | tf_op jit(solution)/shard_map/all_to_all | solution.py:251
  1547.9 424.8 %reduce-scatter.15.cloned.1.call-start = ((), (), s32[]{:S(2)}) async-start(), calls=%async_computation.24 | async-start | bytes 9437184 | tf_op jit(solution)/shard_map/reduce_scatter | solution.py:315
  1826.7 296.7 %reduce-scatter.13.cloned.1.call-start = ((), (), s32[]{:S(2)}) async-start(), calls=%async_computation.23 | async-start | bytes 9437184 | tf_op jit(solution)/shard_map/reduce_scatter | solution.py:309
  1883.6 378.4 %reduce-scatter.31.cloned.1.call-start = ((), (), s32[]{:S(2)}) async-start(), calls=%async_computation.32 | async-start | bytes 1081344
  1887.0 446.1 %reduce-scatter.29.cloned.1.call-start = ((), (), s32[]{:S(2)}) async-start(), calls=%async_computation.31 | async-start | bytes 10485760 | tf_op jit(solution)/shard_map/reduce_scatter | solution.py:261
  1905.1 501.9 %reduce-scatter.25.cloned.1.call-start = ((), (), s32[]{:S(2)}) async-start(), calls=%async_computation.29 | async-start | bytes 10485760 | tf_op jit(solution)/shard_map/reduce_scatter | solution.py:255
  1922.1 558.7 %reduce-scatter.27.cloned.1.call-start = ((), (), s32[]{:S(2)}) async-start(), calls=%async_computation.30 | async-start | bytes 10485760 | tf_op jit(solution)/shard_map/reduce_scatter | solution.py:258
  1939.6 903.5 %reduce-scatter.23.cloned.1.call-start = ((), (), s32[]{:S(2)}) async-start(), calls=%async_computation.28 | async-start | bytes 17301504 | tf_op jit(solution)/shard_map/reduce_scatter | solution.py:359
  1949.6 1253.6 %reduce-scatter.21.cloned.1.call-start = ((), (), s32[]{:S(2)}) async-start(), calls=%async_computation.27 | async-start | bytes 17301504 | tf_op jit(solution)/shard_map/reduce_scatter | solution.py:358
  1984.7 1578.5 %reduce-scatter.19.cloned.1.call-start = ((), (), s32[]{:S(2)}) async-start(), calls=%async_computation.26 | async-start | bytes 17301504 | tf_op jit(solution)/shard_map/reduce_scatter | solution.py:357
  2143.8 1779.7 %reduce-scatter.17.cloned.1.call-start = ((), (), s32[]{:S(2)}) async-start(), calls=%async_computation.25 | async-start | bytes 17301504 | tf_op jit(solution)/shard_map/reduce_scatter | solution.py:356
  (74 other events, 1023.0 us)
Sparse Core Ops, SparseCore 0:
  11.6 79.7 all-gather.16
  94.3 75.6 all-gather.10
  173.6 75.7 all-gather.14
  251.4 123.0 all-gather.18
  376.4 123.1 all-gather.12
  502.4 75.2 all-gather.20
  579.3 56.8 all-gather.22
  637.8 58.2 all-gather.24
  697.6 58.2 all-gather.26
  1826.8 145.9 reduce-scatter.14
  1976.4 146.9 reduce-scatter.12
  2126.1 135.8 reduce-scatter.30
  2264.6 68.5 reduce-scatter.28
  2335.5 71.3 reduce-scatter.24
  2409.4 71.3 reduce-scatter.26
  2483.5 359.4 reduce-scatter.22
  2845.8 357.3 reduce-scatter.20
  3205.9 357.3 reduce-scatter.18
  3566.1 357.3 reduce-scatter.16
where the time goes:
time: 3930 us
  waiting for transfers between devices  2620 us (67%)
  blocking collectives  598 us (15%)
  matrix products  313 us (8%)
  local copies, waits for them, and re-layouts  232 us (6%)
  other arithmetic  125 us (3%)
    reduce_scatter x1, waiting for transfers between devices, per_device(): lax.psum_scatter(grad_query_w, ('grp', 'seq'), scatter_dimension=0, tiled...  360 us
    reduce_scatter x1, waiting for transfers between devices, per_device(): lax.psum_scatter(grad_value_w, ('grp', 'seq'), scatter_dimension=0, tiled...  360 us
    reduce_scatter x1, waiting for transfers between devices, per_device(): lax.psum_scatter(grad_key_w, ('grp', 'seq'), scatter_dimension=0, tiled=T...  360 us
    reduce_scatter x1, waiting for transfers between devices, per_device(): lax.psum_scatter(grad_out_w, ('grp', 'seq'), scatter_dimension=0, tiled=T...  286 us
    all_gather x1, blocking collectives, fetch_attention(): lax.all_gather(router, ('grp', 'seq'), axis=0, tiled=True)  261 us
    all_to_all x1, blocking collectives, per_device(): lax.all_to_all(send_grads, 'seq', split_axis=0, concat_axis=1, tiled=True)  207 us
    all_to_all x1, waiting for transfers between devices, per_device(): lax.all_to_all(send_rows, 'seq', split_axis=0, concat_axis=1, tiled=True)  205 us
    all_to_all x1, waiting for transfers between devices, per_device(): lax.all_to_all(grad_rows, 'seq', split_axis=1, concat_axis=0, tiled=True)  191 us
  transfers between devices with their start and end apart: 22, of which 18 were waited for; matrix products, arithmetic and copies ran while one was open for 10% of the time, Pallas kernels for 0%

commit v1 on v0

v1 whole, which is shorter than its diff:
```python
import functools

import jax
import jax.numpy as jnp
from jax import lax
from jax.experimental import pallas as pl
from jax.experimental.pallas import tpu as pltpu
from jax.sharding import PartitionSpec as P

D = 2048
H = 16
HD = 128
TOP = 8
E = 16
PROMPT = 1024
CONT_LEN = 128

EPSILON = 1e-05
SCALE = HD ** (-0.5)
NEG = -1e30
BLOCK = 256
F32 = jnp.float32
BF16 = jnp.bfloat16


def dot(left, right, dims):
    return lax.dot_general(left, right, (dims, ((), ())), preferred_element_type=F32)


def mm(left, right):
    return dot(left, right, ((1,), (0,)))


def mm_nt(left, right):
    return dot(left, right, ((1,), (1,)))


def mm_tn(left, right):
    return dot(left, right, ((0,), (0,)))


def batched(left, right, left_dim, right_dim):
    return lax.dot_general(
        left, right, (((left_dim,), (right_dim,)), ((0,), (0,))), preferred_element_type=F32
    )


def normalize(values):
    factor = lax.rsqrt(jnp.mean(values * values, axis=-1, keepdims=True) + EPSILON)
    return (values * factor, factor)


def norm_back(grad_normed, normed, factor):
    return factor * (grad_normed - normed * jnp.mean(grad_normed * normed, axis=-1, keepdims=True))


def rotary_tables(total):
    row = jnp.arange(total, dtype=jnp.int32)
    position = jnp.where(row < PROMPT, row, PROMPT + (row - PROMPT) % CONT_LEN)
    inverse_freq = 10000.0 ** (-(jnp.arange(HD // 2, dtype=F32) * 2.0) / HD)
    phase = position.astype(F32)[:, None] * inverse_freq[None, :]
    cosine, sine = jnp.cos(phase), jnp.sin(phase)
    return (
        jnp.concatenate([cosine, cosine], axis=-1),
        jnp.concatenate([-sine, sine], axis=-1),
    )


def prep_kernel(q_in, k_in, v_in, sums, gain_q, gain_k, cos_ref, sin_ref, q_out, k_out, v_out):
    factors = lax.rsqrt(sums[...] * (1.0 / D) + EPSILON)
    cosine, sine = cos_ref[...], sin_ref[...]
    for source, gain, out, col in ((q_in, gain_q, q_out, 0), (k_in, gain_k, k_out, 1)):
        factor = factors[:, col : col + 1]
        for head in range(source.shape[1] // HD):
            cut = slice(head * HD, (head + 1) * HD)
            values = source[:, cut] * factor * gain[:, cut]
            out[:, cut] = (values * cosine + pltpu.roll(values, HD // 2, 1) * sine).astype(BF16)
    v_out[...] = v_in[...].astype(BF16)


def prep(qkv, sums, gain_q, gain_k, cosine, sine):
    total, width = qkv.shape
    cols = width // 3
    rows = pl.BlockSpec((BLOCK, HD), lambda i: (i, 0))

    def part(at):
        return pl.BlockSpec((BLOCK, cols), lambda i: (i, at))

    whole = pl.BlockSpec((1, cols), lambda i: (0, 0))
    return pl.pallas_call(
        prep_kernel,
        grid=(total // BLOCK,),
        in_specs=[
            part(0),
            part(1),
            part(2),
            pl.BlockSpec((BLOCK, 2), lambda i: (i, 0)),
            whole,
            whole,
            rows,
            rows,
        ],
        out_specs=[part(0)] * 3,
        out_shape=[jax.ShapeDtypeStruct((total, cols), BF16)] * 3,
        cost_estimate=pl.CostEstimate(
            flops=8 * total * cols, bytes_accessed=18 * total * cols, transcendentals=0
        ),
        name="qk_prep",
    )(qkv, qkv, qkv, sums, gain_q, gain_k, cosine, sine)


def block_scores(index, query, k_ref):
    keys = k_ref[pl.ds(pl.multiple_of(index * BLOCK, BLOCK), BLOCK), :]
    first = mm_nt(query, k_ref[:PROMPT, :]) * SCALE
    row = index * BLOCK + lax.broadcasted_iota(jnp.int32, first.shape, 0)
    col = lax.broadcasted_iota(jnp.int32, first.shape, 1)
    first = jnp.where(col <= row, first, NEG)
    own = mm_nt(query, keys) * SCALE
    row = lax.broadcasted_iota(jnp.int32, own.shape, 0)
    col = lax.broadcasted_iota(jnp.int32, own.shape, 1)
    seen = (row // CONT_LEN == col // CONT_LEN) & (col <= row) & (index * BLOCK + row >= PROMPT)
    own = jnp.where(seen, own, NEG)
    peak = jnp.maximum(
        jnp.max(first, axis=-1, keepdims=True), jnp.max(own, axis=-1, keepdims=True)
    )
    first = jnp.exp(first - peak)
    own = jnp.exp(own - peak)
    total = jnp.sum(first, axis=-1, keepdims=True) + jnp.sum(own, axis=-1, keepdims=True)
    inverse = 1.0 / total
    return (first * inverse, own * inverse, peak, keys)


def attn_kernel(q_ref, k_ref, v_ref, out_ref, peak_ref):
    index = pl.program_id(1)
    first, own, peak, _ = block_scores(index, q_ref[...], k_ref)
    values = v_ref[pl.ds(pl.multiple_of(index * BLOCK, BLOCK), BLOCK), :]
    mixed = mm(first.astype(BF16), v_ref[:PROMPT, :]) + mm(own.astype(BF16), values)
    out_ref[...] = mixed.astype(BF16)
    highest = jnp.broadcast_to(jnp.max(peak, axis=0, keepdims=True), peak_ref.shape)

    @pl.when(index == 0)
    def _():
        peak_ref[...] = highest

    @pl.when(index > 0)
    def _():
        peak_ref[...] = jnp.maximum(peak_ref[...], highest)


def attn_cost(total, heads, dots):
    pairs = total * (PROMPT + BLOCK) * heads
    return pl.CostEstimate(
        flops=2 * HD * dots * pairs, bytes_accessed=8 * total * heads * HD, transcendentals=pairs
    )


def attention(query, key, value):
    total, cols = query.shape
    heads = cols // HD
    full = pl.BlockSpec((total, HD), lambda h, i: (0, h))
    block = pl.BlockSpec((BLOCK, HD), lambda h, i: (i, h))
    return pl.pallas_call(
        attn_kernel,
        grid=(heads, total // BLOCK),
        in_specs=[block, full, full],
        out_specs=[block, pl.BlockSpec((None, 8, HD), lambda h, i: (h, 0, 0))],
        out_shape=[
            jax.ShapeDtypeStruct((total, cols), BF16),
            jax.ShapeDtypeStruct((heads, 8, HD), F32),
        ],
        cost_estimate=attn_cost(total, heads, 2),
        name="attn_fwd",
    )(query, key, value)


def rotate_back(values, cosine, sine):
    return values * cosine - pltpu.roll(values, HD // 2, 1) * sine


def attn_back_kernel(
    q_ref, k_ref, v_ref, do_ref, cosb_ref, sinb_ref, cos_ref, sin_ref, dq_ref, dk_ref, dv_ref, dk_acc, dv_acc
):
    index = pl.program_id(1)
    here = pl.ds(pl.multiple_of(index * BLOCK, BLOCK), BLOCK)

    @pl.when(index == 0)
    def _():
        dk_acc[...] = jnp.zeros_like(dk_acc)
        dv_acc[...] = jnp.zeros_like(dv_acc)

    query, grad = q_ref[...], do_ref[...]
    first, own, _, keys = block_scores(index, query, k_ref)
    grad_first = mm_nt(grad, v_ref[:PROMPT, :])
    grad_own = mm_nt(grad, v_ref[here, :])
    delta = jnp.sum(first * grad_first, axis=-1, keepdims=True) + jnp.sum(
        own * grad_own, axis=-1, keepdims=True
    )
    grad_first = (first * (grad_first - delta)).astype(BF16)
    grad_own = (own * (grad_own - delta)).astype(BF16)
    first, own = first.astype(BF16), own.astype(BF16)
    dv_acc[:PROMPT, :] += mm_tn(first, grad)
    dv_acc[here, :] += mm_tn(own, grad)
    dk_acc[:PROMPT, :] += mm_tn(grad_first, query)
    dk_acc[here, :] += mm_tn(grad_own, query)
    dq = (mm(grad_first, k_ref[:PROMPT, :]) + mm(grad_own, keys)) * SCALE
    dq_ref[...] = rotate_back(dq, cosb_ref[...], sinb_ref[...])

    @pl.when(index == pl.num_programs(1) - 1)
    def _():
        dk_ref[...] = rotate_back(dk_acc[...] * SCALE, cos_ref[...], sin_ref[...])
        dv_ref[...] = dv_acc[...].astype(BF16)


def attention_back(query, key, value, grad, cosine, sine):
    total, cols = query.shape
    heads = cols // HD
    full = pl.BlockSpec((total, HD), lambda h, i: (0, h))
    block = pl.BlockSpec((BLOCK, HD), lambda h, i: (i, h))
    table = pl.BlockSpec((BLOCK, HD), lambda h, i: (i, 0))
    table_full = pl.BlockSpec((total, HD), lambda h, i: (0, 0))
    return pl.pallas_call(
        attn_back_kernel,
        grid=(heads, total // BLOCK),
        in_specs=[block, full, full, block, table, table, table_full, table_full],
        out_specs=[block, full, full],
        out_shape=[
            jax.ShapeDtypeStruct((total, cols), F32),
            jax.ShapeDtypeStruct((total, cols), F32),
            jax.ShapeDtypeStruct((total, cols), BF16),
        ],
        scratch_shapes=[pltpu.VMEM((total, HD), F32), pltpu.VMEM((total, HD), F32)],
        cost_estimate=attn_cost(total, heads, 5),
        name="attn_back",
    )(query, key, value, grad, cosine, sine, cosine, sine)


def per_device(
    n_grp,
    n_seq,
    tokens,
    cotangent,
    route_ids,
    gain_attn,
    w_query,
    w_key,
    w_value,
    w_out,
    gain_query,
    gain_key,
    gain_ffn,
    router,
    expert_gate,
    expert_up,
    expert_down,
    clip_flags,
    clip_factors,
):
    n_all = n_grp * n_seq
    both = ("grp", "seq")
    rows = tokens.shape[1]
    total = rows * n_seq
    share = D // n_all
    cols = D // n_seq
    heads = H // n_seq
    local_e = E // n_seq
    capacity = 9 * rows * TOP // (8 * E)
    seq = lax.axis_index("seq")
    tokens, cotangent, route_ids = tokens[0], cotangent[0], route_ids[0]

    head_scale = jnp.where(clip_flags == 1, jnp.sqrt(clip_factors), jnp.ones_like(clip_factors))
    column_scale = jnp.broadcast_to(head_scale[:, None], (H, HD)).reshape(D)
    clipped_query = (w_query.astype(F32) * column_scale[None, :]).astype(BF16)
    clipped_key = (w_key.astype(F32) * column_scale[None, :]).astype(BF16)

    tokens_all = lax.all_gather(tokens, "seq", axis=0, tiled=True)

    small = jnp.concatenate(
        [gain_attn[None], gain_query[None], gain_key[None], gain_ffn[None], router.T], axis=0
    ).reshape(1, (4 + E) * share)
    small = lax.all_gather(small, both, axis=0, tiled=True)
    small = small.reshape(n_all, 4 + E, share).transpose(1, 0, 2).reshape(4 + E, D)
    gains = small[:4].astype(F32)
    attn_gain, query_gain, key_gain, ffn_gain = gains[0:1], gains[1:2], gains[2:3], gains[3:4]
    router_t = small[4:]
    query_gain = lax.dynamic_slice(query_gain, (0, seq * cols), (1, cols))
    key_gain = lax.dynamic_slice(key_gain, (0, seq * cols), (1, cols))

    w_qkv = jnp.stack([clipped_query, clipped_key, w_value], axis=1)
    w_qkv = w_qkv.reshape(share, 3, n_seq, cols).transpose(2, 0, 1, 3)
    w_qkv = w_qkv.reshape(n_seq, share, 3 * cols)
    w_qkv = lax.all_to_all(w_qkv, "seq", split_axis=0, concat_axis=0, tiled=True)
    w_qkv = lax.all_gather(w_qkv.reshape(n_seq * share, 3 * cols), "grp", axis=0, tiled=True)

    cosine, sine = rotary_tables(total)

    route_all = lax.all_gather(route_ids, "seq", axis=0, tiled=True).reshape(n_seq, rows, TOP)
    row_at = lax.broadcasted_iota(jnp.int32, (rows, rows), 0)
    col_at = lax.broadcasted_iota(jnp.int32, (rows, rows), 1)
    earlier = (row_at < col_at).astype(BF16)
    slot_at = lax.broadcasted_iota(jnp.int32, (n_seq, capacity, rows), 1)
    picks = []
    for e in range(local_e):
        hit = jnp.any(route_all == seq * local_e + e, axis=-1)
        place = mm(hit.astype(BF16), earlier).astype(jnp.int32)
        picks.append(hit[:, None, :] & (place[:, None, :] == slot_at))

    inputs_all = tokens_all.astype(F32)
    hidden_in = (normalize(inputs_all)[0] * attn_gain).astype(BF16)
    qkv = mm(hidden_in, w_qkv)
    raw_q, raw_k = qkv[:, :cols], qkv[:, cols : 2 * cols]
    sums = jnp.stack([jnp.sum(raw_q * raw_q, axis=-1), jnp.sum(raw_k * raw_k, axis=-1)], axis=0)
    sums = lax.psum(sums, "seq")
    query, key, value = prep(qkv, sums.T, query_gain, key_gain, cosine, sine)
    attended_cols, peaks = attention(query, key, value)
    max_logit = lax.all_gather(peaks[:, 0, 0], "seq", axis=0, tiled=True)
    max_logit = lax.pmax(max_logit, "grp")

    attended = lax.all_to_all(attended_cols, "seq", split_axis=0, concat_axis=1, tiled=True)
    w_out_all = lax.all_gather(w_out, both, axis=0, tiled=True)
    inputs = tokens.astype(F32)
    residual_mid = inputs + mm(attended, w_out_all)
    normed_mid, factor_mid = normalize(residual_mid)
    hidden_mid = (normed_mid * ffn_gain).astype(BF16)
    hidden_all = lax.all_gather(hidden_mid, "seq", axis=0, tiled=True)
    gate_prob = jax.nn.softmax(mm_nt(hidden_mid, router_t), axis=-1)
    gate_prob_all = jax.nn.softmax(mm_nt(hidden_all, router_t), axis=-1)

    gate_w = lax.all_gather(expert_gate, "grp", axis=1, tiled=True)
    up_w = lax.all_gather(expert_up, "grp", axis=1, tiled=True)
    down_w = lax.all_gather(expert_down, "grp", axis=1, tiled=True)
    cotangent_all = lax.all_gather(cotangent, "seq", axis=0, tiled=True)

    hidden_blocks = hidden_all.reshape(n_seq, rows, D)
    cotangent_blocks = cotangent_all.reshape(n_seq, rows, D)
    expert_at = lax.broadcasted_iota(jnp.int32, gate_prob_all.shape, 1)
    mixed_out = jnp.zeros((n_seq, rows, D), F32)
    mixed_grad = jnp.zeros((n_seq, rows, D), F32)
    weight_rows, gate_grads, up_grads, down_grads = [], [], [], []
    for e in range(local_e):
        pick = picks[e].astype(BF16)
        prob = jnp.sum(jnp.where(expert_at == seq * local_e + e, gate_prob_all, 0.0), axis=-1)
        prob = prob.reshape(n_seq, 1, rows)
        weighted = jnp.where(picks[e], prob, 0.0)
        slot_weight = jnp.sum(weighted, axis=-1).reshape(n_seq * capacity, 1)
        received = batched(pick, hidden_blocks, 2, 1).astype(BF16).reshape(n_seq * capacity, D)
        gate_val = mm(received, gate_w[e])
        up_val = mm(received, up_w[e])
        sigmoid_gate = jax.nn.sigmoid(gate_val)
        silu_gate = gate_val * sigmoid_gate
        hidden = (silu_gate * up_val).astype(BF16)
        expert_out = mm(hidden, down_w[e]).astype(BF16)
        out_blocks = expert_out.reshape(n_seq, capacity, D)
        mixed_out = mixed_out + batched(weighted.astype(BF16), out_blocks, 1, 1)

        grad_slot = batched(pick, cotangent_blocks, 2, 1).reshape(n_seq * capacity, D)
        slot_dot = jnp.sum(grad_slot * expert_out.astype(F32), axis=-1)
        slot_dot = slot_dot.reshape(n_seq, capacity, 1)
        weight_rows.append(jnp.sum(jnp.where(picks[e], slot_dot, 0.0), axis=1))
        grad_received = (slot_weight * grad_slot).astype(BF16)
        grad_hidden = mm_nt(grad_received, down_w[e])
        grad_gate = (
            grad_hidden * up_val * sigmoid_gate * (1.0 + gate_val * (1.0 - sigmoid_gate))
        ).astype(BF16)
        grad_up = (grad_hidden * silu_gate).astype(BF16)
        grad_rows = (mm_nt(grad_gate, gate_w[e]) + mm_nt(grad_up, up_w[e])).astype(BF16)
        mixed_grad = mixed_grad + batched(pick, grad_rows.reshape(n_seq, capacity, D), 1, 1)
        down_grads.append(mm_tn(hidden, grad_received).astype(BF16))
        gate_grads.append(mm_tn(received, grad_gate).astype(BF16))
        up_grads.append(mm_tn(received, grad_up).astype(BF16))

    mixed_grad = mixed_grad.reshape(total, D).astype(BF16)
    grad_hidden_mid = lax.psum_scatter(mixed_grad, "seq", scatter_dimension=0, tiled=True)
    mixed_out = mixed_out.reshape(total, D).astype(BF16)
    ffn_out = lax.psum_scatter(mixed_out, "seq", scatter_dimension=0, tiled=True)
    block_out = (residual_mid + ffn_out.astype(F32)).astype(BF16)

    weight_rows = jnp.stack(weight_rows, axis=1)
    weight_rows = lax.all_to_all(weight_rows, "seq", split_axis=0, concat_axis=0, tiled=True)
    grad_prob = weight_rows.reshape(E, rows).T
    grad_logits = gate_prob * (grad_prob - jnp.sum(gate_prob * grad_prob, axis=-1, keepdims=True))
    grad_router = mm_tn(grad_logits, hidden_mid.astype(F32))
    grad_hidden_mid = grad_hidden_mid.astype(F32) + mm(grad_logits, router_t.astype(F32))
    grad_ffn_gain = jnp.sum(grad_hidden_mid * normed_mid, axis=0)
    grad_mid = cotangent.astype(F32) + norm_back(grad_hidden_mid * ffn_gain, normed_mid, factor_mid)
    grad_attn = grad_mid.astype(BF16)
    grad_attended = mm_nt(grad_attn, w_out_all).astype(BF16)
    grad_attended = lax.all_to_all(grad_attended, "seq", split_axis=1, concat_axis=0, tiled=True)

    grad_q, grad_k, grad_v = attention_back(query, key, value, grad_attended, cosine, sine)
    factor_q = lax.rsqrt(sums[0] * (1.0 / D) + EPSILON)[:, None]
    factor_k = lax.rsqrt(sums[1] * (1.0 / D) + EPSILON)[:, None]
    normed_q, normed_k = raw_q * factor_q, raw_k * factor_k
    prod_q, prod_k = grad_q * normed_q, grad_k * normed_k
    grad_query_gain = jnp.sum(prod_q, axis=0)
    grad_key_gain = jnp.sum(prod_k, axis=0)
    means = jnp.stack(
        [jnp.sum(prod_q * query_gain, axis=-1), jnp.sum(prod_k * key_gain, axis=-1)], axis=0
    )
    means = lax.psum(means, "seq") * (1.0 / D)
    grad_q = factor_q * (grad_q * query_gain - normed_q * means[0][:, None])
    grad_k = factor_k * (grad_k * key_gain - normed_k * means[1][:, None])
    grad_qkv = jnp.concatenate([grad_q.astype(BF16), grad_k.astype(BF16), grad_v], axis=1)

    grad_hidden_in = mm_nt(grad_qkv, w_qkv).astype(BF16)
    grad_hidden_in = lax.psum_scatter(grad_hidden_in, "seq", scatter_dimension=0, tiled=True)
    grad_hidden_in = grad_hidden_in.astype(F32)

    grad_w = mm_tn(hidden_in, grad_qkv).astype(BF16)
    grad_w = lax.psum_scatter(grad_w, "grp", scatter_dimension=0, tiled=True)
    grad_w = grad_w.reshape(n_seq, share, 3 * cols)
    grad_w = lax.all_to_all(grad_w, "seq", split_axis=0, concat_axis=0, tiled=True)
    grad_w = grad_w.astype(F32).reshape(n_seq, share, 3, cols).transpose(2, 1, 0, 3)
    grad_w = grad_w.reshape(3, share, D)
    grad_query_w = grad_w[0] * column_scale[None, :]
    grad_key_w = grad_w[1] * column_scale[None, :]
    grad_value_w = grad_w[2]

    grad_attn_all = lax.all_gather(grad_attn, "seq", axis=0, tiled=True)
    attended_own = attended.reshape(rows, n_grp, n_seq, share).transpose(2, 0, 1, 3)
    attended_own = attended_own.reshape(n_seq * rows, n_grp * share)
    attended_own = lax.all_to_all(attended_own, "seq", split_axis=0, concat_axis=0, tiled=True)
    grad_out_w = mm_tn(attended_own, grad_attn_all).astype(BF16)
    grad_out_w = lax.psum_scatter(grad_out_w, "grp", scatter_dimension=0, tiled=True).astype(F32)

    normed_in, factor_in = normalize(inputs)
    grad_attn_gain = jnp.sum(grad_hidden_in * normed_in, axis=0)
    tokens_grad = grad_mid + norm_back(grad_hidden_in * attn_gain, normed_in, factor_in)

    def spread(part):
        return lax.dynamic_update_slice(jnp.zeros((D,), F32), part, (seq * cols,))

    late = jnp.concatenate(
        [
            grad_router,
            grad_ffn_gain[None],
            grad_attn_gain[None],
            spread(grad_query_gain)[None],
            spread(grad_key_gain)[None],
        ],
        axis=0,
    )
    late = late.reshape(E + 4, n_all, share).transpose(1, 0, 2).reshape(n_all, (E + 4) * share)
    late = lax.psum_scatter(late, both, scatter_dimension=0, tiled=True).reshape(E + 4, share)

    def expert_share(parts):
        summed = lax.psum_scatter(jnp.stack(parts), "grp", scatter_dimension=1, tiled=True)
        return summed.astype(F32)

    return (
        block_out[None],
        tokens_grad[None],
        late[E + 1],
        grad_query_w,
        grad_key_w,
        grad_value_w,
        grad_out_w,
        late[E + 2],
        late[E + 3],
        late[E],
        late[:E].T,
        expert_share(gate_grads),
        expert_share(up_grads),
        expert_share(down_grads),
        max_logit,
        clipped_query,
        clipped_key,
    )


def solution(mesh):
    rows = P("grp", "seq", None)
    vector = P(("grp", "seq"))
    matrix = P(("grp", "seq"), None)
    expert = P("seq", "grp", None)
    return jax.shard_map(
        functools.partial(per_device, mesh.shape["grp"], mesh.shape["seq"]),
        mesh=mesh,
        in_specs=(rows, rows, rows, vector)
        + (matrix,) * 4
        + (vector,) * 3
        + (matrix,)
        + (expert,) * 3
        + (P(), P()),
        out_specs=(rows, rows, vector)
        + (matrix,) * 4
        + (vector,) * 3
        + (matrix,)
        + (expert,) * 3
        + (P(), matrix, matrix),
        check_vma=False,
    )
```

time: 3930 us -> 1910 us (0.49)
  waiting for transfers between devices: 2620 us -> 1070 us
  blocking collectives: 598 us -> 305 us
  local copies, waits for them, and re-layouts: 232 us -> 37.7 us
  Pallas kernels: 0 us -> 60.2 us
    reduce_scatter x9 -> x8, waiting for transfers between devices: 1690 us -> 526 us  [the longest x1 149 us: per_device(): lax.psum_scatter(grad_hidden_in, 'seq', scatter_dimension=0, tiled=True)]
    all_to_all x3 -> x4, waiting for transfers between devices: 396 us -> 96.3 us  [the longest x1 50.2 us: per_device(): lax.all_to_all(grad_attended, 'seq', split_axis=1, concat_axis=0, tiled=T...]
    all_gather x1 -> x2, blocking collectives: 261 us -> 102 us  [the longest x1 70.1 us: per_device(): small = lax.all_gather(small, both, axis=0, tiled=True)]
    all_to_all x1 -> x2, blocking collectives: 207 us -> 72.2 us  [the longest x1 49 us: per_device(): lax.all_to_all(w_qkv, 'seq', split_axis=0, concat_axis=0, tiled=True)]
    psum x0 -> x2, blocking collectives: none -> 124 us  [the longest x1 86.7 us: per_device(): sums = lax.psum(sums, 'seq')]
    all_gather x9, waiting for transfers between devices: 429 us -> 318 us  [the longest x1 111 us: per_device(): hidden_all = lax.all_gather(hidden_mid, 'seq', axis=0, tiled=True)]
    unnamed x2 -> x0, blocking collectives: 93.1 us -> none
    gather x5 -> x0, local copies, waits for them, and re-layouts: 76.2 us -> none  [the longest x1 21.2 us: per_device(): route_out = returned[slot_index].reshape(groups, row_count, TOP, D)]
  transfers between devices with their start and end apart: 22 -> 22, of which waited for: 18 -> 17; matrix products, arithmetic and copies ran while one was open for 10% -> 15% of each run, Pallas kernels for 0% -> 3%
where the time goes in v1:
time: 1910 us; the launch traced here: 1900 us
  waiting for transfers between devices  1070 us (56%)
  blocking collectives  305 us (16%)
  matrix products  301 us (16%)
  other arithmetic  92.5 us (5%)
  Pallas kernels  60.2 us (3%)
  local copies, waits for them, and re-layouts  37.7 us (2%)
    dot_general x30, matrix products, dot(): lax.dot_general(left, right, (dims, ((), ())), preferred_element_type=F32)  229 us
    reduce_scatter x1, waiting for transfers between devices, per_device(): lax.psum_scatter(grad_hidden_in, 'seq', scatter_dimension=0, tiled=True)  149 us
    reduce_scatter x1, waiting for transfers between devices, per_device(): lax.psum_scatter(mixed_out, 'seq', scatter_dimension=0, tiled=True)  143 us
    reduce_scatter x1, waiting for transfers between devices, per_device(): lax.psum_scatter(mixed_grad, 'seq', scatter_dimension=0, tiled=True)  134 us
    unnamed x19, waiting for transfers between devices  127 us
    all_gather x1, waiting for transfers between devices, per_device(): hidden_all = lax.all_gather(hidden_mid, 'seq', axis=0, tiled=True)  111 us
    reduce_scatter x3, waiting for transfers between devices, expert_share(): lax.psum_scatter(jnp.stack(parts), 'grp', scatter_dimension=1, tiled=True)  92.9 us
    psum x1, blocking collectives, per_device(): sums = lax.psum(sums, 'seq')  86.7 us
  transfers between devices with their start and end apart: 22, of which 17 were waited for; matrix products, arithmetic and copies ran while one was open for 15% of the time, Pallas kernels for 3%

profile of v1, /device:TPU:0, one launch (start us, length us, event | category | flops | bytes accessed | tf_op | source)
XLA Modules:
  0.0 1897.9 jit_solution(4773415068030965604)
XLA Ops:
  15.2 49.0 %all_to_all.65 = bf16[8,64,768]{2,1,0:T(8,128)(2,1)} all-to-all(bf16[8,64,768]{2,1,0:T(8,128)(2,1)S(1)} %reshape.281), channel_id=1, replica_groups=mesh['grp'=4,'seq'=8] {'seq'}, dimensions={0} | all-to-all | bytes 1572864 | tf_op jit(solution)/shard_map/all_to_all | solution.py:291
  65.9 70.1 %all-gather.4 = bf16[32,1,1280]{2,1,0:T(2,128)(2,1)S(1)} all-gather(bf16[1,1,1280]{2,1,0:T(2,128)(2,1)S(1)} %reshape.314), channel_id=1, replica_groups=mesh['grp'=4,'seq'=8] {'grp','seq'}, dimensions={0}, use_global_device_ids=true | all-gather | bytes 84480 | tf_op jit(solution)/shard_map/all_gather | solution.py:280
  143.4 13.5 all-gather.29.cloned.1.call-done
  161.9 23.3 %all-gather.15.cloned.1.call-done = bf16[2048,768]{1,0:T(8,128)(2,1)} async-done(((bf16[512,768]{1,0:T(8,128)(2,1)}), bf16[2048,768]{1,0:T(8,128)(2,1)}) %all-gather.15.cloned.1.call-update) | async-done | bytes 3145744 | tf_op jit(solution)/shard_map/all_gather | solution.py:292
  199.1 86.7 %psum.14 = f32[2,2048]{0,1:T(8,128)} all-reduce(f32[2,2048]{0,1:T(8,128)S(1)} %copy.82), channel_id=1, replica_groups=mesh['grp'=4,'seq'=8] {'seq'}, use_global_device_ids=true, to_apply=%region_3.4 | all-reduce | flops 4096 | bytes 32768 | tf_op jit(solution)/shard_map/psum | solution.py:312
  294.2 19.3 %attn_fwd.1 = (bf16[2048,256]{1,0:T(8,128)(2,1)}, f32[2,8,128]{2,1,0:T(8,128)}) custom-call(bf16[2048,256]{1,0:T(8,128)(2,1)} %get-tuple-element.25.q_ref, bf16[2048,256]{1,0:T(8,128)(2,1)} %get-tuple-element.26.k_ref, bf16[2048,256]{1,0:T(8,128)(2,1)} %get-tuple-element.27.v_ref), custom_call_target="tpu_custom_call" | custom-call | flops 2684354560 | bytes 4194304 | tf_op jit(solution)/shard_map/attn_fwd/pallas_call | solution.py:162
  319.7 39.3 %all-to-all-done.1 = bf16[8,256,256]{1,2,0:T(8,128)(2,1)S(1)} async-done(((bf16[8,256,256]{1,2,0:T(8,128)(2,1)}), bf16[8,256,256]{1,2,0:T(8,128)(2,1)S(1)}, u32[]{:S(2)}, u32[]{:S(2)}) %all-to-all-start.1) | async-done | bytes 1048608 | tf_op jit(solution)/shard_map/all_to_all | solution.py:318
  369.9 32.1 %all-gather.1 = s32[1,2048,8]{1,2,0:T(8,128)S(1)} all-gather(s32[1,256,8]{1,2,0:T(8,128)S(1)} %copy-done.56), channel_id=3, replica_groups=mesh['grp'=4,'seq'=8] {'seq'}, dimensions={1}, use_global_device_ids=true | all-gather | bytes 73728 | tf_op jit(solution)/shard_map/all_gather | solution.py:296
  402.7 34.4 %all-gather.31.cloned.1.call-done = bf16[1,2048,2048]{2,1,0:T(8,128)(2,1)} async-done(((bf16[1,256,2048]{2,1,0:T(8,128)(2,1)}), bf16[1,2048,2048]{2,1,0:T(8,128)(2,1)}) %all-gather.31.cloned.1.call-update) | async-done | bytes 8388624 | tf_op jit(solution)/shard_map/all_gather | solution.py:331
  450.9 110.9 %all-gather.19.cloned.1.call-done = bf16[2048,2048]{1,0:T(8,128)(2,1)} async-done(((bf16[256,2048]{1,0:T(8,128)(2,1)}), bf16[2048,2048]{1,0:T(8,128)(2,1)}) %all-gather.19.cloned.1.call-update) | async-done | bytes 8388624 | tf_op jit(solution)/shard_map/all_gather | solution.py:324
  582.8 36.9 %all-gather.21.cloned.1.call-done = bf16[2,2048,1024]{2,1,0:T(8,128)(2,1)} async-done(((bf16[2,512,1024]{2,1,0:T(8,128)(2,1)}), bf16[2,2048,1024]{2,1,0:T(8,128)(2,1)}) %all-gather.21.cloned.1.call-update) | async-done | bytes 8388624 | tf_op jit(solution)/shard_map/all_gather | solution.py:328
  629.6 50.0 %all-gather.23.cloned.1.call-done = bf16[2,2048,1024]{2,1,0:T(8,128)(2,1)} async-done(((bf16[2,512,1024]{2,1,0:T(8,128)(2,1)}), bf16[2,2048,1024]{2,1,0:T(8,128)(2,1)}) %all-gather.23.cloned.1.call-update) | async-done | bytes 8388624 | tf_op jit(solution)/shard_map/all_gather | solution.py:329
  679.6 10.9 multiply_convert_fusion.7
  690.5 49.0 %all-gather.25.cloned.1.call-done = bf16[2,1024,2048]{2,1,0:T(8,128)(2,1)} async-done(((bf16[2,256,2048]{2,1,0:T(8,128)(2,1)}), bf16[2,1024,2048]{2,1,0:T(8,128)(2,1)}) %all-gather.25.cloned.1.call-update) | async-done | bytes 8388624 | tf_op jit(solution)/shard_map/all_gather | solution.py:330
  739.4 10.4 fusion.5
  788.1 12.1 multiply_convert_fusion.4
  825.3 11.4 multiply_convert_fusion.2
  852.2 11.8 add_convert_fusion
  878.7 134.1 %reduce-scatter.11.cloned.1.call-done = bf16[256,2048]{1,0:T(8,128)(2,1)} async-done(((bf16[2048,2048]{1,0:T(8,128)(2,1)}), bf16[256,2048]{1,0:T(8,128)(2,1)}) %reduce-scatter.11.cloned.1.call-update) | async-done | bytes 1048592 | tf_op jit(solution)/shard_map/reduce_scatter | solution.py:372
  1032.6 50.2 %all-to-all-done.3 = bf16[256,8,256]{2,0,1:T(8,128)(2,1)S(1)} async-done(((bf16[256,8,256]{2,0,1:T(8,128)(2,1)}), bf16[256,8,256]{2,0,1:T(8,128)(2,1)S(1)}, u32[]{:S(2)}, u32[]{:S(2)}) %all-to-all-start.3) | async-done | bytes 1048608 | tf_op jit(solution)/shard_map/all_to_all | solution.py:387
  1083.7 32.5 %attn_back.1 = (f32[2048,256]{1,0:T(8,128)}, f32[2048,256]{1,0:T(8,128)}, bf16[2048,256]{1,0:T(8,128)(2,1)}) custom-call(bf16[2048,256]{1,0:T(8,128)(2,1)} %get-tuple-element.25.q_ref, bf16[2048,256]{1,0:T(8,128)(2,1)} %get-tuple-element.26.k_ref, bf16[2048,256]{1,0:T(8,128)(2,1)} %get-tuple-element.27.v_ref, bf16[2048,256]{1,0:T(8,128)(2,1)} %bitcast.274, ...), custom_call_target="tpu_custom_call" | custom-call | flops 6710886400 | bytes 4194304 | tf_op jit(solution)/shard_map/attn_back/pallas_call | solution.py:221
  1120.9 37.1 %all-reduce.2 = (f32[2,2048]{1,0:T(2,128)S(1)}, f32[16]{0:T(128)S(1)}) all-reduce(f32[2,2048]{1,0:T(2,128)S(1)} %pad_maximum_fusion.10, f32[16]{0:T(128)S(1)} %dynamic-update-slice), channel_id=1, replica_groups=mesh['grp'=4,'seq'=8] {'seq'}, use_global_device_ids=true, to_apply=%region_26.27 | all-reduce | flops 4112 | bytes 32896 | tf_op jit(solution)/shard_map/psum | solution.py:399
  1163.4 11.0 convolution_convert_fusion.5
  1257.8 23.2 %all_to_all.66 = bf16[8,256,256]{1,2,0:T(8,128)(2,1)S(1)} all-to-all(bf16[8,256,256]{1,2,0:T(8,128)(2,1)S(1)} %bitcast.263), channel_id=1, replica_groups=mesh['grp'=4,'seq'=8] {'seq'}, dimensions={0} | all-to-all | bytes 2097152 | tf_op jit(solution)/shard_map/all_to_all | solution.py:421
  1288.6 11.2 convolution_convert_fusion.2
  1300.6 11.3 fusion.50
  1311.9 11.7 add_convert_fusion.1
  1334.5 23.1 %reduce-scatter.19.cloned.1.call-done = bf16[2,512,1024]{2,1,0:T(8,128)(2,1)} async-done(((bf16[2,2048,1024]{2,1,0:T(8,128)(2,1)}), bf16[2,512,1024]{2,1,0:T(8,128)(2,1)}) %reduce-scatter.19.cloned.1.call-update) | async-done | bytes 2097168 | tf_op jit(solution)/shard_map/reduce_scatter | solution.py:446
  1361.7 69.8 %reduce-scatter.21.cloned.1.call-done = bf16[2,512,1024]{2,1,0:T(8,128)(2,1)} async-done(((bf16[2,2048,1024]{2,1,0:T(8,128)(2,1)}), bf16[2,512,1024]{2,1,0:T(8,128)(2,1)}) %reduce-scatter.21.cloned.1.call-update) | async-done | bytes 2097168 | tf_op jit(solution)/shard_map/reduce_scatter | solution.py:446
  1460.5 149.2 %reduce-scatter.13.cloned.1.call-done = bf16[256,2048]{1,0:T(8,128)(2,1)} async-done(((bf16[2048,2048]{1,0:T(8,128)(2,1)}), bf16[256,2048]{1,0:T(8,128)(2,1)}) %reduce-scatter.13.cloned.1.call-update) | async-done | bytes 1048592 | tf_op jit(solution)/shard_map/reduce_scatter | solution.py:405
  1616.3 143.5 %reduce-scatter.9.cloned.1.call-done = bf16[256,2048]{1,0:T(8,128)(2,1)} async-done(((bf16[2048,2048]{1,0:T(8,128)(2,1)}), bf16[256,2048]{1,0:T(8,128)(2,1)}) %reduce-scatter.9.cloned.1.call-update) | async-done | bytes 1048592 | tf_op jit(solution)/shard_map/reduce_scatter | solution.py:374
  1765.1 122.7 %all-reduce.5.cloned.1.call-done = f32[32,1280]{1,0:T(8,128)} async-done(((f32[32,1280]{1,0:T(8,128)}), f32[32,1280]{1,0:T(8,128)}) %all-reduce.5.cloned.1.call-update) | async-done | bytes 163856
  (375 shorter events, 379.3 us)
Async XLA Ops:
  7.2 149.6 %all-gather.29.cloned.1.call-start = ((), (), s32[]{:S(2)}) async-start(), calls=%async_computation.29 | async-start | bytes 9437184 | tf_op jit(solution)/shard_map/all_gather | solution.py:275
  7.9 177.3 %all-gather.15.cloned.1.call-start = ((), (), s32[]{:S(2)}) async-start(), calls=%async_computation.14 | async-start | bytes 3932160 | tf_op jit(solution)/shard_map/all_gather | solution.py:292
  64.2 255.4 %all-gather.17.cloned.1.call-start = ((), (), s32[]{:S(2)}) async-start(), calls=%async_computation.15 | async-start | bytes 8650752 | tf_op jit(solution)/shard_map/all_gather | solution.py:319
  65.0 372.2 %all-gather.31.cloned.1.call-start = ((), (), s32[]{:S(2)}) async-start(), calls=%async_computation.30 | async-start | bytes 9437184 | tf_op jit(solution)/shard_map/all_gather | solution.py:331
  315.8 43.2 %all-to-all-start.1 = ((bf16[8,256,256]{1,2,0:T(8,128)(2,1)}), bf16[8,256,256]{1,2,0:T(8,128)(2,1)S(1)}, u32[]{:S(2)}, u32[]{:S(2)}) async-start(bf16[8,256,256]{1,2,0:T(8,128)(2,1)} %copy.86), calls=%async_computation.1 | async-start | bytes 2097152 | tf_op jit(solution)/shard_map/all_to_all | solution.py:318
  319.5 242.3 %all-gather.19.cloned.1.call-start = ((), (), s32[]{:S(2)}) async-start(), calls=%async_computation.16 | async-start | bytes 9437184 | tf_op jit(solution)/shard_map/all_gather | solution.py:324
  367.8 252.0 %all-gather.21.cloned.1.call-start = ((), (), s32[]{:S(2)}) async-start(), calls=%async_computation.17 | async-start | bytes 10485760 | tf_op jit(solution)/shard_map/all_gather | solution.py:328
  368.3 311.3 %all-gather.23.cloned.1.call-start = ((), (), s32[]{:S(2)}) async-start(), calls=%async_computation.18 | async-start | bytes 10485760 | tf_op jit(solution)/shard_map/all_gather | solution.py:329
  369.1 370.4 %all-gather.25.cloned.1.call-start = ((), (), s32[]{:S(2)}) async-start(), calls=%async_computation.19 | async-start | bytes 10485760 | tf_op jit(solution)/shard_map/all_gather | solution.py:330
  369.8 643.0 %reduce-scatter.11.cloned.1.call-start = ((), (), s32[]{:S(2)}) async-start(), calls=%async_computation.21 | async-start | bytes 9437184 | tf_op jit(solution)/shard_map/reduce_scatter | solution.py:372
  402.2 415.0 %copy-start.24 = (pred[8,256]{1,0:T(8,128)(4,1)}, pred[8,256]{1,0:T(8,128)(4,1)S(1)}, u32[]{:S(2)}) copy-start(pred[8,256]{1,0:T(8,128)(4,1)S(1)} %and.40) | copy-start | bytes 6148
  402.4 159.4 %copy-start.17 = (bf16[16,2048]{1,0:T(8,128)(2,1)}, bf16[16,2048]{1,0:T(8,128)(2,1)S(1)}, u32[]{:S(2)}) copy-start(bf16[16,2048]{1,0:T(8,128)(2,1)S(1)} %slice.119) | copy-start | bytes 196612
  402.6 414.6 %copy-start.15 = (s32[8,256]{1,0:T(8,128)}, s32[8,256]{1,0:T(8,128)S(1)}, u32[]{:S(2)}) copy-start(s32[8,256]{1,0:T(8,128)S(1)} %convolution_convert_fusion.9) | copy-start | bytes 24580
  567.7 215.3 %copy-start.37 = (f32[8,256]{1,0:T(8,128)}, f32[8,256]{1,0:T(8,128)S(1)}, u32[]{:S(2)}) copy-start(f32[8,256]{1,0:T(8,128)S(1)} %broadcast_in_dim.108) | copy-start | bytes 24580
  567.7 182.2 %copy-start.28 = (f32[8,256]{1,0:T(8,128)}, f32[8,256]{1,0:T(8,128)S(1)}, u32[]{:S(2)}) copy-start(f32[8,256]{1,0:T(8,128)S(1)} %broadcast_in_dim.105) | copy-start | bytes 24580
  865.6 152.9 %copy-start.26 = (f32[256,16]{0,1:T(8,128)}, f32[256,16]{0,1:T(8,128)S(1)}, u32[]{:S(2)}) copy-start(f32[256,16]{0,1:T(8,128)S(1)} %get-tuple-element.98) | copy-start | bytes 49156
  865.6 152.9 %copy-start.44 = (f32[256]{0:T(256)}, f32[256]{0:T(256)S(1)}, u32[]{:S(2)}) copy-start(f32[256]{0:T(256)S(1)} %get-tuple-element.97) | copy-start | bytes 3076
  866.2 12.4 all-to-all-start.2
  871.8 409.8 %all-gather.27.cloned.1.call-start = ((), (), s32[]{:S(2)}) async-start(), calls=%async_computation.24 | async-start | bytes 9437184 | tf_op jit(solution)/shard_map/all_gather | solution.py:418
  1025.7 57.1 %all-to-all-start.3 = ((bf16[256,8,256]{2,0,1:T(8,128)(2,1)}), bf16[256,8,256]{2,0,1:T(8,128)(2,1)S(1)}, u32[]{:S(2)}, u32[]{:S(2)}) async-start(bf16[256,8,256]{2,0,1:T(8,128)(2,1)} %bitcast.229), calls=%async_computation.5 | async-start | bytes 2097152 | tf_op jit(solution)/shard_map/all_to_all | solution.py:387
  1029.4 294.2 %reduce-scatter.15.cloned.1.call-start = ((), (), s32[]{:S(2)}) async-start(), calls=%async_computation.23 | async-start | bytes 3932160 | tf_op jit(solution)/shard_map/reduce_scatter | solution.py:409
  1174.5 155.9 %reduce-scatter.23.cloned.1.call-start = ((), (), s32[]{:S(2)}) async-start(), calls=%async_computation.28 | async-start | bytes 10485760 | tf_op jit(solution)/shard_map/reduce_scatter | solution.py:446
  1207.0 150.6 %reduce-scatter.19.cloned.1.call-start = ((), (), s32[]{:S(2)}) async-start(), calls=%async_computation.26 | async-start | bytes 10485760 | tf_op jit(solution)/shard_map/reduce_scatter | solution.py:446
  1232.2 199.3 %reduce-scatter.21.cloned.1.call-start = ((), (), s32[]{:S(2)}) async-start(), calls=%async_computation.27 | async-start | bytes 10485760 | tf_op jit(solution)/shard_map/reduce_scatter | solution.py:446
  1256.5 202.2 %reduce-scatter.17.cloned.1.call-start = ((), (), s32[]{:S(2)}) async-start(), calls=%async_computation.25 | async-start | bytes 1310720 | tf_op jit(solution)/shard_map/reduce_scatter | solution.py:423
  1288.5 321.1 %reduce-scatter.13.cloned.1.call-start = ((), (), s32[]{:S(2)}) async-start(), calls=%async_computation.22 | async-start | bytes 9437184 | tf_op jit(solution)/shard_map/reduce_scatter | solution.py:405
  1299.9 459.9 %reduce-scatter.9.cloned.1.call-start = ((), (), s32[]{:S(2)}) async-start(), calls=%async_computation.20 | async-start | bytes 9437184 | tf_op jit(solution)/shard_map/reduce_scatter | solution.py:374
  1323.6 121.6 %all-to-all-start.4 = ((bf16[8,64,768]{2,1,0:T(8,128)(2,1)}), bf16[8,64,768]{2,1,0:T(8,128)(2,1)}, u32[]{:S(2)}, u32[]{:S(2)}) async-start(bf16[8,64,768]{2,1,0:T(8,128)(2,1)} %bitcast.279), calls=%async_computation.8 | async-start | bytes 1572864 | tf_op jit(solution)/shard_map/all_to_all | solution.py:411
  1328.0 559.7 %all-reduce.5.cloned.1.call-start = ((), (), s32[]{:S(2)}) async-start(), calls=%async_computation.31 | async-start | bytes 327680
  1328.4 281.2 %copy-start.54 = (f32[256]{0:T(256)}, f32[256]{0:T(256)S(1)}, u32[]{:S(2)}) copy-start(f32[256]{0:T(256)S(1)} %add_rsqrt_fusion.1) | copy-start | bytes 3076
  1450.9 308.9 %copy-start.4 = (f32[256,2048]{1,0:T(8,128)S(1)}, f32[256,2048]{1,0:T(8,128)}, u32[]{:S(2)}) copy-start(f32[256,2048]{1,0:T(8,128)} %copy-done.2) | copy-start | bytes 6291460
  1450.9 308.9 %copy-start.34 = (f32[2048]{0:T(1024)S(1)}, f32[2048]{0:T(1024)}, u32[]{:S(2)}) copy-start(f32[2048]{0:T(1024)} %copy-done.32) | copy-start | bytes 24580
  (78 other events, 2045.1 us)
Sparse Core Ops, SparseCore 0:
  10.1 146.6 all-gather.28
  158.4 26.8 all-gather.14
  188.2 99.5 all-gather.16
  289.9 147.2 all-gather.30
  439.1 122.6 all-gather.18
  563.2 56.4 all-gather.20
  621.3 58.2 all-gather.22
  681.1 58.2 all-gather.24
  864.1 148.7 reduce-scatter.10
  1018.6 146.6 all-gather.26
  1174.6 35.1 reduce-scatter.14
  1212.2 71.3 reduce-scatter.22
  1286.2 71.3 reduce-scatter.18
  1360.0 71.3 reduce-scatter.20
  1433.8 24.8 reduce-scatter.16
  1462.2 147.4 reduce-scatter.12
  1613.1 146.5 reduce-scatter.8
  1765.1 122.5 all-reduce.4
